TPU v7x, 512 devices: a whole 4x8x8 slice. The times are simulated.
512 devices in a mesh: space: 64 (over x, y, z_lo), mode: 8 (over z_hi, core).
Axes of the slice: x: 4, y: 8, z: 8 (z_hi: 4, z_lo: 2; z = z_hi * 2 + z_lo), core: 2. Of those that a mesh axis runs over, the one named last changes fastest.
Arguments:
- state: float32 [858, 65536], P(None, ('space', 'mode')), may hold values from -6 to 6
- tensor: bfloat16 [64, 286, 858], P('mode'), may hold values from -0.01171875 to 0.01171875
- table: int32 [286, 3], replicated, may hold values from 0 to 10, as said below
- thermal: float32 [3], replicated, may hold values from 0.5 to 2
- output_mode_row: int32 [64], replicated, may hold values from 0 to 857, as said below
Outputs:
- updated: float32 [858, 65536], P(None, ('space', 'mode'))
- collision: float32 [64, 65536], P('mode', 'space')
Inputs may be any that keep to these rules, and one draw needn't show every extreme that they name: `table`: each row holds the three indices of one multi-index of total degree at most 10; every such multi-index is in exactly one row. `output_mode_row`: all entries are different.
All inputs are finite; a program needn't handle non-finite values.
Results may differ from a plain program's by a relative error of at most 0.004.
Values may be sent and summed in bfloat16 or wider, within the bound.
A program may use at most 64 MiB of HBM per device.

v0:
```python
import jax
import jax.numpy as jnp
from jax import lax
from jax.sharding import PartitionSpec as P

CLASSES = 3
MODES = 286
wave_bound = 5.2
courant = 0.09
collision_update = 0.1


def extended_2(x, sides, width):
    for axis, dim in sides:
        size, length = (lax.axis_size(axis), x.shape[dim])
        up = [(i, (i + 1) % size) for i in range(size)]
        down = [(j, i) for i, j in up]
        last = lax.slice_in_dim(x, length - width, length, axis=dim)
        first = lax.slice_in_dim(x, 0, width, axis=dim)
        before = lax.ppermute(last, axis, up)
        after = lax.ppermute(first, axis, down)
        x = jnp.concatenate([before, x, after], axis=dim)
    return x


def advection_matrix(table):
    codes = table[:, 0] * 144 + table[:, 1] * 12 + table[:, 2]
    along = table[:, 0].astype(jnp.float32)
    lower = (codes[None, :] == codes[:, None] - 144).astype(jnp.float32)
    higher = (codes[None, :] == codes[:, None] + 144).astype(jnp.float32)
    return jnp.sqrt(along)[:, None] * lower + jnp.sqrt(along + 1.0)[:, None] * higher


def upwind_transport(extended, state, matrix, thermal):
    blocks = extended.reshape(CLASSES, MODES, -1)
    state_after_collision = jnp.einsum(
        "ab,cbx->cax", matrix, blocks, precision=lax.Precision.HIGHEST
    )
    speed = thermal[:, None, None]
    flux = 0.5 * speed * (
        state_after_collision[:, :, :-1] + state_after_collision[:, :, 1:]
    ) - 0.5 * wave_bound * speed * (blocks[:, :, 1:] - blocks[:, :, :-1])
    change = (flux[:, :, 1:] - flux[:, :, :-1]).reshape(CLASSES * MODES, -1)
    return state - courant * change


def shards(state, tensor, table, thermal, output_mode_row):
    per_device = tensor.shape[0]
    own_modes = lax.dynamic_slice_in_dim(
        output_mode_row, lax.axis_index("mode") * per_device, per_device
    )
    mode_selector = ((own_modes // MODES)[:, None] == jnp.arange(CLASSES)[None, :]).astype(
        jnp.float32
    )
    flat = tensor.reshape(per_device * MODES, CLASSES * MODES)
    matrix = advection_matrix(table)
    piece = lax.all_gather(state.astype(jnp.bfloat16), "mode", axis=1, tiled=True)
    width = piece.shape[1]
    product = jnp.dot(flat, piece, preferred_element_type=jnp.float32).reshape(
        per_device, MODES, width
    )
    first = jnp.einsum(
        "oc,cix->oix", mode_selector, piece.reshape(CLASSES, MODES, width).astype(jnp.float32)
    )
    collision = jnp.sum(first * product, axis=1)
    extended = extended_2(state, ((("space", "mode"), 1),), 1)
    advected_state = upwind_transport(extended, state, matrix, thermal)
    own_terms = lax.all_to_all(
        collision.astype(jnp.bfloat16), "mode", split_axis=1, concat_axis=0, tiled=True
    ).astype(collision.dtype)
    placing = (jnp.arange(CLASSES * MODES)[:, None] == output_mode_row[None, :]).astype(jnp.float32)
    collision_increment = jnp.dot(
        placing, own_terms, precision=lax.Precision.HIGHEST, preferred_element_type=jnp.float32
    )
    updated = advected_state + collision_update * collision_increment
    return (updated, collision)


def solution(mesh):
    in_specs = (P(None, ("space", "mode")), P("mode", None, None), P(), P(), P())
    out_specs = (P(None, ("space", "mode")), P("mode", "space"))
    return jax.shard_map(shards, mesh=mesh, in_specs=in_specs, out_specs=out_specs, check_vma=False)
```

profile of v0, /device:TPU:4, one launch (start us, length us, event | category | flops | bytes accessed | tf_op | source)
XLA Modules:
  0.0 88.0 jit_solution(16369945874256971813)
XLA Ops:
  7.2 1.7 %convert_element_type.22 = bf16[858,128]{1,0:T(8,128)(2,1)} convert(f32[858,128]{1,0:T(8,128)} %param.5) | non-fusion elementwise | flops 109824 | bytes 658944 | tf_op jit(solution)/shard_map/convert_element_type | solution.py:57
  9.0 1.3 %fusion.26 = (f32[858,1]{1,0:T(8,128)S(1)}, f32[858,1]{1,0:T(8,128)S(1)}) fusion(f32[858,128]{1,0:T(8,128)} %param.5), kind=kLoop, calls=%fused_computation.42 | loop fusion | bytes 13728 | tf_op jit(solution)/shard_map/slice | solution.py:18
  10.3 1.9 %collective-permute-start = (f32[858,1]{1,0:T(8,128)S(1)}, f32[858,1]{1,0:T(8,128)S(1)}, u32[]{:S(2)}, u32[]{:S(2)}) collective-permute-start(f32[858,1]{1,0:T(8,128)S(1)} %get-tuple-element.9), channel_id=1, source_target_pairs={{0,1},{1,2},{2,3},{3,4},{4,5},{5,6},{6,7},{7,8},{8,9},{9,10},{10,1... | collective-permute-start | bytes 10304 | tf_op jit(solution)/shard_map/ppermute | solution.py:20
  12.2 13.3 %collective-permute-start.1 = (f32[858,1]{1,0:T(8,128)S(1)}, f32[858,1]{1,0:T(8,128)S(1)}, u32[]{:S(2)}, u32[]{:S(2)}) collective-permute-start(f32[858,1]{1,0:T(8,128)S(1)} %get-tuple-element.10), channel_id=1, source_target_pairs={{1,0},{2,1},{3,2},{4,3},{5,4},{6,5},{7,6},{8,7},{9,8},{10,9},{11,1... | collective-permute-start | bytes 10304 | tf_op jit(solution)/shard_map/ppermute | solution.py:21
  25.5 0.7 sqrt_reduce_fusion.1
  26.2 0.8 add_reduce_fusion.1
  27.0 0.7 broadcast_multiply_fusion.1
  27.7 0.7 and_select_fusion
  28.4 3.0 %collective-permute-done = f32[858,1]{1,0:T(8,128)S(1)} collective-permute-done((f32[858,1]{1,0:T(8,128)S(1)}, f32[858,1]{1,0:T(8,128)S(1)}, u32[]{:S(2)}, u32[]{:S(2)}) %collective-permute-start) | collective-permute-done | bytes 3464 | tf_op jit(solution)/shard_map/ppermute | solution.py:20
  31.4 1.4 %collective-permute-done.1 = f32[858,1]{1,0:T(8,128)S(1)} collective-permute-done((f32[858,1]{1,0:T(8,128)S(1)}, f32[858,1]{1,0:T(8,128)S(1)}, u32[]{:S(2)}, u32[]{:S(2)}) %collective-permute-start.1) | collective-permute-done | bytes 3464 | tf_op jit(solution)/shard_map/ppermute | solution.py:21
  32.8 1.4 %pad_maximum_fusion = f32[858,130]{1,0:T(8,128)S(1)} fusion(f32[858,1]{1,0:T(8,128)S(1)} %collective-permute-done.1, f32[858,128]{1,0:T(8,128)} %param.5, f32[858,1]{1,0:T(8,128)S(1)} %collective-permute-done), kind=kLoop, calls=%fused_computation.7 | loop fusion | flops 223080 | bytes 892320 | tf_op jit(solution)/shard_map/concatenate | solution.py:22
  34.3 0.3 fusion.25
  34.6 0.3 copy.22
  34.9 0.3 copy.21
  35.3 3.6 %convolution_bitcast_fusion = f32[3,286,130]{1,2,0:T(8,128)S(1)} fusion(f32[3,286,130]{2,1,0:T(8,128)S(1)} %reshape.57, f32[286]{0:T(512)S(1)} %get-tuple-element.3, f32[286]{0:T(512)S(1)} %get-tuple-element.2, s32[286]{0:T(512)S(1)} %get-tuple-element.6, s32[286]{0:T(512)S(1)} %get-tuple-element.5, s32[286]{0:T(512)S(1)} %get-tuple-element.4), kind=kOutput, calls=%fused_computation.4 | convolution fusion | flops 383214272 | bytes 898040 | tf_op jit(solution)/shard_map/ab,cbx->cax/dot_general | solution.py:36
  39.1 16.5 %all-gather.2.cloned.1.call-done = bf16[858,1024]{1,0:T(8,128)(2,1)} async-done(((bf16[858,128]{1,0:T(8,128)(2,1)}), bf16[858,1024]{1,0:T(8,128)(2,1)}) %all-gather.2.cloned.1.call-update) | async-done | bytes 1757200 | tf_op jit(solution)/shard_map/all_gather | solution.py:57
  55.6 1.9 %reshape.53 = bf16[3,286,1024]{2,1,0:T(8,128)(2,1)S(1)} reshape(bf16[858,1024]{1,0:T(8,128)(2,1)} %all-gather.2.cloned.1.call-done) | data formatting | bytes 3514368 | tf_op jit(solution)/shard_map/reshape | solution.py:63
  57.5 1.8 %fusion = f32[8,286,1024]{2,0,1:T(8,128)S(1)} fusion(bf16[3,286,1024]{2,1,0:T(8,128)(2,1)S(1)} %reshape.53, s32[8]{0:T(128)S(1)} %and_select_fusion), kind=kOutput, calls=%fused_computation.1 | convolution fusion | flops 14057496 | bytes 11128864 | tf_op jit(solution)/shard_map/oc,cix->oix/dot_general | solution.py:62
  59.3 0.9 copy-done.4
  60.2 5.4 %multiply_reduce_fusion = f32[8,1024]{1,0:T(8,128)S(1)} fusion(f32[8,286,1024]{2,0,1:T(8,128)S(1)} %fusion, bf16[8,286,858]{2,0,1:T(8,128)(2,1)S(1)} %copy-done.4, bf16[858,1024]{1,0:T(8,128)(2,1)S(1)} %copy-done.1), kind=kOutput, calls=%fused_computation | convolution fusion | flops 4025114624 | bytes 15087808 | tf_op jit(solution)/shard_map/dot_general | solution.py:59
  65.6 0.6 convert_bitcast_fusion
  66.2 6.2 %all-to-all-start = ((bf16[8,8,128]{2,0,1:T(8,128)(2,1)}), bf16[8,8,128]{2,0,1:T(8,128)(2,1)S(1)}, u32[]{:S(2)}, u32[]{:S(2)}) async-start(bf16[8,8,128]{2,0,1:T(8,128)(2,1)} %convert_bitcast_fusion), calls=%async_computation | async-start | bytes 32768 | tf_op jit(solution)/shard_map/all_to_all | solution.py:68
  72.7 7.4 %all-to-all-done = bf16[8,8,128]{2,0,1:T(8,128)(2,1)S(1)} async-done(((bf16[8,8,128]{2,0,1:T(8,128)(2,1)}), bf16[8,8,128]{2,0,1:T(8,128)(2,1)S(1)}, u32[]{:S(2)}, u32[]{:S(2)}) %all-to-all-start) | async-done | bytes 16416 | tf_op jit(solution)/shard_map/all_to_all | solution.py:68
  80.2 1.0 %fusion.3 = f32[858,128]{1,0:T(8,128)} fusion(f32[858,128]{1,0:T(8,128)S(1)} %copy-done, f32[858,128]{1,0:T(8,128)S(1)} %mul.109, s32[64]{0:T(128)S(1)} %copy-done.3, bf16[8,8,128]{2,0,1:T(8,128)(2,1)S(1)} %all-to-all-done), kind=kOutput, calls=%fused_computation.6 | convolution fusion | flops 14441856 | bytes 1334528 | tf_op jit(solution)/shard_map/dot_general | solution.py:72
  (16 shorter events, 0.7 us)
Async XLA Ops:
  7.2 48.4 %all-gather.2.cloned.1.call-start = ((), (), s32[]{:S(2)}) async-start(), calls=%async_computation.1 | async-start | bytes 1990656 | tf_op jit(solution)/shard_map/all_gather | solution.py:57
  10.3 21.1 %collective-permute-start = (f32[858,1]{1,0:T(8,128)S(1)}, f32[858,1]{1,0:T(8,128)S(1)}, u32[]{:S(2)}, u32[]{:S(2)}) collective-permute-start(f32[858,1]{1,0:T(8,128)S(1)} %get-tuple-element.9), channel_id=1, source_target_pairs={{0,1},{1,2},{2,3},{3,4},{4,5},{5,6},{6,7},{7,8},{8,9},{9,10},{10,1... | collective-permute-start | bytes 10304 | tf_op jit(solution)/shard_map/ppermute | solution.py:20
  12.2 20.6 %collective-permute-start.1 = (f32[858,1]{1,0:T(8,128)S(1)}, f32[858,1]{1,0:T(8,128)S(1)}, u32[]{:S(2)}, u32[]{:S(2)}) collective-permute-start(f32[858,1]{1,0:T(8,128)S(1)} %get-tuple-element.10), channel_id=1, source_target_pairs={{1,0},{2,1},{3,2},{4,3},{5,4},{6,5},{7,6},{8,7},{9,8},{10,9},{11,1... | collective-permute-start | bytes 10304 | tf_op jit(solution)/shard_map/ppermute | solution.py:21
  57.5 1.8 %copy-start.1 = (bf16[858,1024]{1,0:T(8,128)(2,1)S(1)}, bf16[858,1024]{1,0:T(8,128)(2,1)}, u32[]{:S(2)}) copy-start(bf16[858,1024]{1,0:T(8,128)(2,1)} %all-gather.2.cloned.1.call-done) | copy-start | bytes 5271556
  57.5 2.7 %copy-start.4 = (bf16[8,286,858]{2,0,1:T(8,128)(2,1)S(1)}, bf16[8,286,858]{2,0,1:T(8,128)(2,1)}, u32[]{:S(2)}) copy-start(bf16[8,286,858]{2,0,1:T(8,128)(2,1)} %param.6) | copy-start | bytes 11778628
  60.2 20.0 %copy-start = (f32[858,128]{1,0:T(8,128)S(1)}, f32[858,128]{1,0:T(8,128)}, u32[]{:S(2)}) copy-start(f32[858,128]{1,0:T(8,128)} %param.5) | copy-start | bytes 1317892
  60.2 20.0 %copy-start.3 = (s32[64]{0:T(128)S(1)}, s32[64]{0:T(128)}, u32[]{:S(2)}) copy-start(s32[64]{0:T(128)} %param.9) | copy-start | bytes 772
  65.6 15.6 %copy-start.2 = (f32[8,1024]{1,0:T(8,128)}, f32[8,1024]{1,0:T(8,128)S(1)}, u32[]{:S(2)}) copy-start(f32[8,1024]{1,0:T(8,128)S(1)} %multiply_reduce_fusion) | copy-start | bytes 98308
  66.2 14.0 %all-to-all-start = ((bf16[8,8,128]{2,0,1:T(8,128)(2,1)}), bf16[8,8,128]{2,0,1:T(8,128)(2,1)S(1)}, u32[]{:S(2)}, u32[]{:S(2)}) async-start(bf16[8,8,128]{2,0,1:T(8,128)(2,1)} %convert_bitcast_fusion), calls=%async_computation | async-start | bytes 32768 | tf_op jit(solution)/shard_map/all_to_all | solution.py:68
Sparse Core Ops, SparseCore 0:
  10.7 44.8 all-gather.1
where the time goes:
time: 88.5 us; the launch traced here: 88 us
  waiting for transfers between devices  28.3 us (32%)
  starting transfers between devices  21.4 us (24%)
  between operations  14.2 us (16%)
  matrix products  11.8 us (13%)
  other arithmetic  6.99 us (8%)
  local copies, waits for them, and re-layouts  5.42 us (6%)
    all_gather x1, waiting for transfers between devices, shards(): lax.all_gather(state.astype(jnp.bfloat16), 'mode', axis=1, tiled=True)  16.5 us
    ppermute x1, starting transfers between devices, extended_2(): after = lax.ppermute(first, axis, down)  13.3 us
    all_to_all x1, waiting for transfers between devices, shards(): lax.all_to_all(collision.astype(jnp.bfloat16), 'mode', split_axis=1, conc...  7.44 us
    all_to_all x1, starting transfers between devices, shards(): lax.all_to_all(collision.astype(jnp.bfloat16), 'mode', split_axis=1, conc...  6.19 us
    dot_general x1, matrix products, shards(): jnp.dot(flat, piece, preferred_element_type=jnp.float32)  5.41 us
    dot_general x1, matrix products, upwind_transport(): jnp.einsum('ab,cbx->cax', matrix, blocks, precision=lax.Precision.HIGHEST)  3.58 us
    ppermute x1, waiting for transfers between devices, extended_2(): before = lax.ppermute(last, axis, up)  2.96 us
    ppermute x1, starting transfers between devices, extended_2(): before = lax.ppermute(last, axis, up)  1.92 us
  transfers between devices with their start and end apart: 4, of which 4 were waited for; matrix products, arithmetic and copies ran while one was open for 12% of the time, Pallas kernels for 0%

commit v1 on v0

--- a/solution.py
+++ b/solution.py
@@ -54,7 +54,12 @@
     )
     flat = tensor.reshape(per_device * MODES, CLASSES * MODES)
     matrix = advection_matrix(table)
-    piece = lax.all_gather(state.astype(jnp.bfloat16), "mode", axis=1, tiled=True)
+    piece = jnp.concatenate(
+        lax.all_to_all(
+            jnp.stack([state.astype(jnp.bfloat16)] * lax.axis_size("mode")), "mode", 0, 0
+        ),
+        axis=1,
+    )
     width = piece.shape[1]
     product = jnp.dot(flat, piece, preferred_element_type=jnp.float32).reshape(
         per_device, MODES, width

time: 88.5 us -> 115 us (1.30)
  the two profiles are of different devices: /device:TPU:4 before, /device:TPU:96 now
where the time goes in v1:
time: 115 us; the launch traced here: 114 us
  waiting for transfers between devices  51.4 us (45%)
  starting transfers between devices  21.3 us (19%)
  local copies, waits for them, and re-layouts  17 us (15%)
  matrix products  13.4 us (12%)
  other arithmetic  10.1 us (9%)
    ppermute x1, waiting for transfers between devices, extended_2(): before = lax.ppermute(last, axis, up)  44 us
    all_to_all x1, starting transfers between devices, shards(): lax.all_to_all(jnp.stack([state.astype(jnp.bfloat16)] * lax.axis_size('mo...  9.41 us
    all_to_all x1, waiting for transfers between devices, shards(): lax.all_to_all(collision.astype(jnp.bfloat16), 'mode', split_axis=1, conc...  7.36 us
    ppermute x1, starting transfers between devices, extended_2(): after = lax.ppermute(first, axis, down)  6.16 us
    unnamed x22, local copies, waits for them, and re-layouts  5.97 us
    dot_general x1, matrix products, shards(): jnp.dot(flat, piece, preferred_element_type=jnp.float32)  5.45 us
    reshape x2, local copies, waits for them, and re-layouts, shards(): jnp.concatenate(lax.all_to_all(jnp.stack([state.astype(jnp.bfloat16)] * l...  4.12 us
    dot_general x1, matrix products, upwind_transport(): jnp.einsum('ab,cbx->cax', matrix, blocks, precision=lax.Precision.HIGHEST)  3.57 us
  transfers between devices with their start and end apart: 4, of which 2 were waited for; matrix products, arithmetic and copies ran while one was open for 17% of the time, Pallas kernels for 0%

profile of v1, /device:TPU:96, one launch (start us, length us, event | category | flops | bytes accessed | tf_op | source)
XLA Modules:
  0.0 114.0 jit_solution(9065194865861547311)
XLA Ops:
  0.6 1.0 convert_element_type.22
  1.7 1.5 %stack.2 = bf16[8,858,128]{2,1,0:T(8,128)(2,1)} broadcast(bf16[858,128]{1,0:T(8,128)(2,1)S(1)} %convert_element_type.22), dimensions={1,2} | broadcast | bytes 1976832 | tf_op jit(solution)/shard_map/stack | solution.py:59
  3.1 9.4 %all-to-all-start = ((bf16[8,858,128]{2,1,0:T(8,128)(2,1)}), bf16[8,858,128]{2,1,0:T(8,128)(2,1)S(1)}, u32[]{:S(2)}, u32[]{:S(2)}) async-start(bf16[8,858,128]{2,1,0:T(8,128)(2,1)} %stack.2), calls=%async_computation | async-start | bytes 3538944 | tf_op jit(solution)/shard_map/all_to_all | solution.py:58
  12.7 2.4 %collective-permute-start = (f32[858,1]{1,0:T(8,128)S(1)}, f32[858,1]{1,0:T(8,128)S(1)}, u32[]{:S(2)}, u32[]{:S(2)}) collective-permute-start(f32[858,1]{1,0:T(8,128)S(1)} %get-tuple-element.9), channel_id=1, source_target_pairs={{0,1},{1,2},{2,3},{3,4},{4,5},{5,6},{6,7},{7,8},{8,9},{9,10},{10,1... | collective-permute-start | bytes 10304 | tf_op jit(solution)/shard_map/ppermute | solution.py:20
  15.2 6.2 %collective-permute-start.1 = (f32[858,1]{1,0:T(8,128)S(1)}, f32[858,1]{1,0:T(8,128)}, u32[]{:S(2)}, u32[]{:S(2)}) collective-permute-start(f32[858,1]{1,0:T(8,128)S(1)} %get-tuple-element.10), channel_id=1, source_target_pairs={{1,0},{2,1},{3,2},{4,3},{5,4},{6,5},{7,6},{8,7},{9,8},{10,9},{11,1... | collective-permute-start | bytes 10304 | tf_op jit(solution)/shard_map/ppermute | solution.py:21
  22.1 1.4 %add_reduce_fusion.1 = (s32[286]{0:T(512)S(1)}, s32[286]{0:T(512)S(1)}, s32[286]{0:T(512)}) fusion(s32[286,3]{0,1:T(4,128)} %param.7), kind=kLoop, calls=%fused_computation.34 | loop fusion | flops 1716 | bytes 6864 | tf_op jit(solution)/shard_map/sub | solution.py:29
  23.5 1.2 %broadcast_multiply_fusion.1 = (f32[3]{0:T(128)}, f32[3]{0:T(128)}) fusion(f32[3]{0:T(128)} %param.8), kind=kLoop, calls=%fused_computation.38 | loop fusion | flops 6 | bytes 36 | tf_op jit(solution)/shard_map/mul | solution.py:40
  24.6 1.2 %and_select_fusion = s32[8]{0:T(128)} fusion(s32[64]{0:T(128)} %param.9, s32[]{:T(128)S(6)} %select_n.8), kind=kLoop, calls=%fused_computation.30 | loop fusion | flops 64 | bytes 68 | tf_op jit(solution)/shard_map/jit(floor_divide)/jit(_where)/select_n | solution.py:52
  25.9 44.0 %collective-permute-done = f32[858,1]{1,0:T(8,128)S(1)} collective-permute-done((f32[858,1]{1,0:T(8,128)S(1)}, f32[858,1]{1,0:T(8,128)S(1)}, u32[]{:S(2)}, u32[]{:S(2)}) %collective-permute-start) | collective-permute-done | bytes 3464 | tf_op jit(solution)/shard_map/ppermute | solution.py:20
  69.9 2.3 %pad_maximum_fusion = f32[858,130]{1,0:T(8,128)} fusion(f32[858,1]{1,0:T(8,128)} %collective-permute-done.1, f32[858,128]{1,0:T(8,128)S(1)} %copy-done, f32[858,1]{1,0:T(8,128)S(1)} %collective-permute-done), kind=kLoop, calls=%fused_computation.6 | loop fusion | flops 223080 | bytes 892320 | tf_op jit(solution)/shard_map/concatenate | solution.py:22
  72.2 1.3 %reshape.64 = f32[3,286,130]{2,1,0:T(8,128)S(1)} reshape(f32[858,130]{1,0:T(8,128)} %pad_maximum_fusion) | data formatting | bytes 892320 | tf_op jit(solution)/shard_map/reshape | solution.py:35
  73.5 1.5 %fusion.24 = (f32[3,286,129]{2,1,0:T(8,128)}, f32[3,286,129]{2,1,0:T(8,128)}) fusion(f32[3,286,130]{2,1,0:T(8,128)S(1)} %reshape.64), kind=kLoop, calls=%fused_computation.40 | loop fusion | bytes 1770912 | tf_op jit(solution)/shard_map/slice | solution.py:42
  75.0 2.4 %copy.31 = f32[3,286,129]{1,2,0:T(8,128)} copy(f32[3,286,129]{2,1,0:T(8,128)} %get-tuple-element.8) | data formatting | bytes 885456
  77.4 2.3 %copy.32 = f32[3,286,129]{1,2,0:T(8,128)} copy(f32[3,286,129]{2,1,0:T(8,128)} %get-tuple-element.7) | data formatting | bytes 885456
  79.7 3.6 %convolution_bitcast_fusion = f32[3,286,130]{1,2,0:T(8,128)S(1)} fusion(f32[3,286,130]{2,1,0:T(8,128)S(1)} %reshape.64, f32[286]{0:T(512)S(1)} %get-tuple-element.3, f32[286]{0:T(512)S(1)} %get-tuple-element.2, s32[286]{0:T(512)S(1)} %copy-done.4, s32[286]{0:T(512)S(1)} %get-tuple-element.5, s32[286]{0:T(512)S(1)} %get-tuple-element.4), kind=kOutput, calls=%fused_computation.3 | convolution fusion | flops 383214272 | bytes 898040 | tf_op jit(solution)/shard_map/ab,cbx->cax/dot_general | solution.py:36
  83.3 1.5 %fusion.4 = f32[3,286,129]{1,2,0:T(8,128)S(1)} fusion(f32[3,286,130]{1,2,0:T(8,128)S(1)} %convolution_bitcast_fusion, f32[3,286,129]{1,2,0:T(8,128)} %copy.31, f32[3,286,129]{1,2,0:T(8,128)} %copy.32, f32[3]{0:T(128)S(1)} %copy-done.8, f32[3]{0:T(128)S(1)} %copy-done.7), kind=kLoop, calls=%fused_computation.9 | loop fusion | flops 553410 | bytes 2213664 | tf_op jit(solution)/shard_map/sub | solution.py:40
  84.8 1.2 %copy-done.1 = bf16[8,858,128]{2,1,0:T(8,128)(2,1)} copy-done((bf16[8,858,128]{2,1,0:T(8,128)(2,1)}, bf16[8,858,128]{2,1,0:T(8,128)(2,1)S(1)}, u32[]{:S(2)}) %copy-start.1) | copy-done | bytes 1757208
  86.0 2.2 %copy.22 = bf16[858,8,128]{2,1,0:T(8,128)(2,1)S(1)} copy(bf16[858,8,128]{2,0,1:T(8,128)(2,1)} %bitcast.19) | data formatting | bytes 3514368 | tf_op jit(solution)/shard_map/reshape | solution.py:57
  88.2 2.3 %reshape_reshape.3 = bf16[3,286,1024]{2,1,0:T(8,128)(2,1)} reshape(bf16[858,8,128]{2,1,0:T(8,128)(2,1)S(1)} %copy.22) | data formatting | bytes 3514368 | tf_op jit(solution)/shard_map/reshape;reshape | solution.py:68
  90.4 2.0 %reshape.62 = bf16[858,1024,1]{1,0,2:T(8,128)(2,1)} reshape(bf16[858,8,128]{2,1,0:T(8,128)(2,1)S(1)} %copy.22) | data formatting | bytes 3514368 | tf_op jit(solution)/shard_map/reshape | solution.py:57
  92.4 3.4 %fusion = f32[8,286,1024]{2,0,1:T(8,128)S(1)} fusion(bf16[3,286,1024]{2,1,0:T(8,128)(2,1)} %reshape_reshape.3, s32[8]{0:T(128)S(1)} %copy-done.6), kind=kOutput, calls=%fused_computation.1 | convolution fusion | flops 14057496 | bytes 11128864 | tf_op jit(solution)/shard_map/oc,cix->oix/dot_general | solution.py:67
  95.9 5.5 %multiply_reduce_fusion = f32[8,1024]{1,0:T(8,128)S(1)} fusion(f32[8,286,1024]{2,0,1:T(8,128)S(1)} %fusion, bf16[8,286,858]{2,0,1:T(8,128)(2,1)S(1)} %copy-done.9, bf16[858,1024,1]{1,0,2:T(8,128)(2,1)S(1)} %copy-done.2), kind=kOutput, calls=%fused_computation | convolution fusion | flops 4025114624 | bytes 15087808 | tf_op jit(solution)/shard_map/dot_general | solution.py:64
  102.0 3.3 %all-to-all-start.1 = ((bf16[8,8,128]{2,0,1:T(8,128)(2,1)}), bf16[8,8,128]{2,0,1:T(8,128)(2,1)S(1)}, u32[]{:S(2)}, u32[]{:S(2)}) async-start(bf16[8,8,128]{2,0,1:T(8,128)(2,1)} %convert_bitcast_fusion), calls=%async_computation.1 | async-start | bytes 32768 | tf_op jit(solution)/shard_map/all_to_all | solution.py:73
  105.6 7.4 %all-to-all-done.1 = bf16[8,8,128]{2,0,1:T(8,128)(2,1)S(1)} async-done(((bf16[8,8,128]{2,0,1:T(8,128)(2,1)}), bf16[8,8,128]{2,0,1:T(8,128)(2,1)S(1)}, u32[]{:S(2)}, u32[]{:S(2)}) %all-to-all-start.1) | async-done | bytes 16416 | tf_op jit(solution)/shard_map/all_to_all | solution.py:73
  (28 shorter events, 2.9 us)
Async XLA Ops:
  1.7 10.9 %copy-start = (f32[858,128]{1,0:T(8,128)S(1)}, f32[858,128]{1,0:T(8,128)}, u32[]{:S(2)}) copy-start(f32[858,128]{1,0:T(8,128)} %param.5) | copy-start | bytes 1317892
  3.1 81.6 %all-to-all-start = ((bf16[8,858,128]{2,1,0:T(8,128)(2,1)}), bf16[8,858,128]{2,1,0:T(8,128)(2,1)S(1)}, u32[]{:S(2)}, u32[]{:S(2)}) async-start(bf16[8,858,128]{2,1,0:T(8,128)(2,1)} %stack.2), calls=%async_computation | async-start | bytes 3538944 | tf_op jit(solution)/shard_map/all_to_all | solution.py:58
  12.7 57.1 %collective-permute-start = (f32[858,1]{1,0:T(8,128)S(1)}, f32[858,1]{1,0:T(8,128)S(1)}, u32[]{:S(2)}, u32[]{:S(2)}) collective-permute-start(f32[858,1]{1,0:T(8,128)S(1)} %get-tuple-element.9), channel_id=1, source_target_pairs={{0,1},{1,2},{2,3},{3,4},{4,5},{5,6},{6,7},{7,8},{8,9},{9,10},{10,1... | collective-permute-start | bytes 10304 | tf_op jit(solution)/shard_map/ppermute | solution.py:20
  15.2 54.7 %collective-permute-start.1 = (f32[858,1]{1,0:T(8,128)S(1)}, f32[858,1]{1,0:T(8,128)}, u32[]{:S(2)}, u32[]{:S(2)}) collective-permute-start(f32[858,1]{1,0:T(8,128)S(1)} %get-tuple-element.10), channel_id=1, source_target_pairs={{1,0},{2,1},{3,2},{4,3},{5,4},{6,5},{7,6},{8,7},{9,8},{10,9},{11,1... | collective-permute-start | bytes 10304 | tf_op jit(solution)/shard_map/ppermute | solution.py:21
  75.0 4.7 %copy-start.4 = (s32[286]{0:T(512)S(1)}, s32[286]{0:T(512)}, u32[]{:S(2)}) copy-start(s32[286]{0:T(512)} %get-tuple-element.6) | copy-start | bytes 3436
  75.0 8.3 %copy-start.7 = (f32[3]{0:T(128)S(1)}, f32[3]{0:T(128)}, u32[]{:S(2)}) copy-start(f32[3]{0:T(128)} %get-tuple-element.11) | copy-start | bytes 40
  75.0 8.3 %copy-start.8 = (f32[3]{0:T(128)S(1)}, f32[3]{0:T(128)}, u32[]{:S(2)}) copy-start(f32[3]{0:T(128)} %get-tuple-element.12) | copy-start | bytes 40
  84.8 1.2 %copy-start.1 = (bf16[8,858,128]{2,1,0:T(8,128)(2,1)}, bf16[8,858,128]{2,1,0:T(8,128)(2,1)S(1)}, u32[]{:S(2)}) copy-start(bf16[8,858,128]{2,1,0:T(8,128)(2,1)S(1)} %all-to-all-done) | copy-start | bytes 5271556
  90.4 2.0 %copy-start.6 = (s32[8]{0:T(128)S(1)}, s32[8]{0:T(128)}, u32[]{:S(2)}) copy-start(s32[8]{0:T(128)} %and_select_fusion) | copy-start | bytes 100
  92.4 3.4 %copy-start.2 = (bf16[858,1024,1]{1,0,2:T(8,128)(2,1)S(1)}, bf16[858,1024,1]{1,0,2:T(8,128)(2,1)}, u32[]{:S(2)}) copy-start(bf16[858,1024,1]{1,0,2:T(8,128)(2,1)} %reshape.62) | copy-start | bytes 5271556
  92.4 3.4 %copy-start.9 = (bf16[8,286,858]{2,0,1:T(8,128)(2,1)S(1)}, bf16[8,286,858]{2,0,1:T(8,128)(2,1)}, u32[]{:S(2)}) copy-start(bf16[8,286,858]{2,0,1:T(8,128)(2,1)} %param.6) | copy-start | bytes 11778628
  101.3 12.7 %copy-start.3 = (f32[8,1024]{1,0:T(8,128)}, f32[8,1024]{1,0:T(8,128)S(1)}, u32[]{:S(2)}) copy-start(f32[8,1024]{1,0:T(8,128)S(1)} %multiply_reduce_fusion) | copy-start | bytes 98308
  101.3 11.7 %copy-start.5 = (s32[64]{0:T(128)S(1)}, s32[64]{0:T(128)}, u32[]{:S(2)}) copy-start(s32[64]{0:T(128)} %param.9) | copy-start | bytes 772
  102.0 11.0 %all-to-all-start.1 = ((bf16[8,8,128]{2,0,1:T(8,128)(2,1)}), bf16[8,8,128]{2,0,1:T(8,128)(2,1)S(1)}, u32[]{:S(2)}, u32[]{:S(2)}) async-start(bf16[8,8,128]{2,0,1:T(8,128)(2,1)} %convert_bitcast_fusion), calls=%async_computation.1 | async-start | bytes 32768 | tf_op jit(solution)/shard_map/all_to_all | solution.py:73
